TPU v7x, 32 devices: a whole 2x2x4 slice. The times are simulated.
32 devices in a mesh: gx: 4 (over x, core), gy: 8 (over z, y).
Axes of the slice: x: 2, y: 2, z: 4, core: 2. Of those that a mesh axis runs over, the one named last changes fastest.
Arguments:
- loads: bfloat16 [4, 8, 1024, 128], P('gx', 'gy'), may hold values from -6 to 6
- initial_guess: float32 [4, 8, 1024, 128], P('gx', 'gy'), may hold values from -3 to 3
- local_inverse: bfloat16 [4, 8, 1024, 1024], P('gx', 'gy'), may hold values from -0.25 to 1.25
- diag_coef: float32 [4, 8, 1024], P('gx', 'gy'), may hold values from 1 to 4
- couplings: float32 [4, 8, 1024], P('gx', 'gy'), may hold values from 0.2 to 0.6
- interface_rows: int32 [4, 8, 1024], P('gx', 'gy'), may hold values from 0 to 1023, each once within a row
- owned_mask: int32 [4, 8, 1024], P('gx', 'gy'), may hold values 0 or 1
- coarse_modes: float32 [4, 8, 1024, 6], P('gx', 'gy'), may hold values from -0.125 to 0.125
- coarse_inverse: bfloat16 [192, 192], P(('gx', 'gy')), may hold values from -0.875 to 0.875
Outputs:
- solution: float32 [4, 8, 1024, 128], P('gx', 'gy')
All inputs are finite; a program needn't handle non-finite values. No bound on the sum of `owned_mask` on one device may be relied on, other than what follows from the above.
Results may differ from a plain program's by a relative error of at most 0.0033.
Values may be sent and summed in bfloat16 or wider, within the bound.
A program may use at most 64 MiB of HBM per device.

v0:
```python
import jax
import jax.numpy as jnp
from jax import lax
from jax.sharding import PartitionSpec as P

IR = 128


def shifted(shard, axis, by):
    peers = lax.axis_size(axis)
    pairs = [(i, i + by) for i in range(peers) if 0 <= i + by < peers]
    return lax.ppermute(shard, axis, pairs)


def apply_operator(field, scaling, coupling, row_order):
    side_order = row_order[: 4 * IR]
    interface_values = field[side_order].reshape(4, IR, field.shape[1])
    from_below = shifted(interface_values[1], "gx", 1)
    from_above = shifted(interface_values[0], "gx", -1)
    from_left = shifted(interface_values[3], "gy", 1)
    from_right = shifted(interface_values[2], "gy", -1)
    received = jnp.concatenate([from_below, from_above, from_left, from_right], 0)
    placed = jnp.zeros(field.shape, jnp.float32).at[side_order].set(received)
    return scaling * field - coupling * placed


def coarse_solve(coarse_res, owner_rows):
    grid_row = lax.all_gather(coarse_res, "gy", axis=0, tiled=True)
    return jnp.dot(
        owner_rows,
        lax.all_gather(grid_row, "gx", axis=0, tiled=True),
        preferred_element_type=jnp.float32,
    )


def body(
    loads,
    initial_guess,
    local_inverse,
    diag_coef,
    couplings,
    interface_rows,
    owned_mask,
    coarse_modes,
    coarse_inverse,
):
    load_values = loads[0, 0].astype(jnp.float32)
    inverse = local_inverse[0, 0]
    scaling = diag_coef[0, 0][:, None]
    coupling = couplings[0, 0][:, None]
    row_order = interface_rows[0, 0]
    owned = owned_mask[0, 0].astype(jnp.float32)[:, None]
    modes_local = coarse_modes[0, 0]
    solution = initial_guess[0, 0]
    residual = load_values - apply_operator(solution, scaling, coupling, row_order)
    residual_half = residual.astype(jnp.bfloat16)
    local_step = owned * jnp.dot(inverse, residual_half, preferred_element_type=jnp.float32)
    coarse_res = jnp.dot(modes_local.T, residual, precision=lax.Precision.HIGHEST).astype(
        jnp.bfloat16
    )
    coarse_coef = coarse_solve(coarse_res, coarse_inverse)
    correction = jnp.dot(modes_local, coarse_coef, precision=lax.Precision.HIGHEST)
    solution = solution + local_step + correction
    return solution[None, None]


def solution(mesh):
    return jax.shard_map(
        body,
        mesh=mesh,
        in_specs=(
            P("gx", "gy", None, None),
            P("gx", "gy", None, None),
            P("gx", "gy", None, None),
            P("gx", "gy", None),
            P("gx", "gy", None),
            P("gx", "gy", None),
            P("gx", "gy", None),
            P("gx", "gy", None, None),
            P(("gx", "gy"), None),
        ),
        out_specs=P("gx", "gy", None, None),
        check_vma=False,
    )
```

profile of v0, /device:TPU:0, one launch (start us, length us, event | category | flops | bytes accessed | tf_op | source)
XLA Modules:
  0.0 57.8 jit_solution(14119277289220441979)
XLA Ops:
  0.0 0.0 copy-start
  0.0 0.0 copy-start.1
  0.0 0.8 %compare_select_fusion = s32[512,1]{0,1:T(1,128)S(1)} fusion(s32[1,1,1024]{2,1,0:T(1,128)} %param.14), kind=kLoop, calls=%fused_computation.31 | loop fusion | flops 1536 | bytes 4096 | tf_op jit(solution)/shard_map/select_n | solution.py:23
  0.9 0.0 copy-start.6
  0.9 2.1 %gather_fusion = f32[512,128]{1,0:T(8,128)S(1)} fusion(f32[1024,128]{1,0:T(8,128)} %bitcast.58, s32[1024]{0:T(1024)S(1)} %pad_clamp_fusion), kind=kCustom, calls=%fused_computation | custom fusion | bytes 526336 | tf_op jit(solution)/shard_map/gather | solution.py:17
  3.0 0.0 copy-start.2
  3.0 0.0 copy-start.3
  3.0 0.0 copy-start.4
  3.0 0.7 %fusion.31 = (f32[128,128]{1,0:T(8,128)}, f32[128,128]{1,0:T(8,128)}, f32[128,128]{1,0:T(8,128)}, f32[128,128]{1,0:T(8,128)}) fusion(f32[512,128]{1,0:T(8,128)S(1)} %gather_fusion), kind=kLoop, calls=%fused_computation.33 | loop fusion | bytes 524288 | tf_op jit(solution)/shard_map/slice | solution.py:18
  3.7 1.3 %collective-permute-start.3 = (f32[128,128]{1,0:T(8,128)}, f32[128,128]{1,0:T(8,128)S(1)}, u32[]{:S(2)}, u32[]{:S(2)}) collective-permute-start(f32[128,128]{1,0:T(8,128)} %get-tuple-element.8), channel_id=1, source_target_pairs={{1,0},{2,1},{3,2},{4,3},{5,4},{6,5},{7,6},{9,8},{10,9},{11,10},{12... | collective-permute-start | bytes 196616 | tf_op jit(solution)/shard_map/ppermute | solution.py:12
  5.0 6.2 %collective-permute-start.2 = (f32[128,128]{1,0:T(8,128)}, f32[128,128]{1,0:T(8,128)}, u32[]{:S(2)}, u32[]{:S(2)}) collective-permute-start(f32[128,128]{1,0:T(8,128)} %get-tuple-element.6), channel_id=1, source_target_pairs={{0,1},{1,2},{2,3},{3,4},{4,5},{5,6},{6,7},{8,9},{9,10},{10,11},{11... | collective-permute-start | bytes 196616 | tf_op jit(solution)/shard_map/ppermute | solution.py:12
  11.1 1.3 %collective-permute-start.1 = (f32[128,128]{1,0:T(8,128)}, f32[128,128]{1,0:T(8,128)}, u32[]{:S(2)}, u32[]{:S(2)}) collective-permute-start(f32[128,128]{1,0:T(8,128)} %get-tuple-element.7), channel_id=1, source_target_pairs={{8,0},{16,8},{24,16},{9,1},{17,9},{25,17},{10,2},{18,10},{26,18},{... | collective-permute-start | bytes 196616 | tf_op jit(solution)/shard_map/ppermute | solution.py:12
  12.4 3.7 %collective-permute-start = (f32[128,128]{1,0:T(8,128)}, f32[128,128]{1,0:T(8,128)}, u32[]{:S(2)}, u32[]{:S(2)}) collective-permute-start(f32[128,128]{1,0:T(8,128)} %get-tuple-element.5), channel_id=1, source_target_pairs={{0,8},{8,16},{16,24},{1,9},{9,17},{17,25},{2,10},{10,18},{18,26},{... | collective-permute-start | bytes 196616 | tf_op jit(solution)/shard_map/ppermute | solution.py:12
  16.1 0.0 copy-done.1
  16.1 0.2 copy.23
  16.3 1.1 %copy.24 = bf16[1,1,1024,128]{2,3,1,0:T(8,128)(2,1)S(1)} copy(bf16[1,1,1024,128]{3,2,1,0:T(8,128)(2,1)} %param.9) | data formatting | bytes 524288 | tf_op args[0]
  17.4 0.0 copy-done.6
  17.4 0.0 collective-permute-done.3
  17.4 0.0 collective-permute-done.2
  17.4 0.0 collective-permute-done.1
  17.4 0.0 collective-permute-done
  17.5 2.9 %scatter_custom_fusion = f32[1024,128]{1,0:T(8,128)} fusion(s32[512]{0:T(512)S(1)} %bitcast.65, f32[128,128]{1,0:T(8,128)S(1)} %collective-permute-done.3, f32[]{:T(128)} %constant.15, f32[128,128]{1,0:T(8,128)} %collective-permute-done.2, f32[128,128]{1,0:T(8,128)} %collective-permute-done.1, f32[128,128]{1,0:T(8,128)} %collective-permute-done, ...), kind=kCustom, calls=%fused_computation.15 | custom fusion | flops 196608 | bytes 786440 | tf_op jit(solution)/shard_map/scatter | solution.py:23
  20.3 1.2 %copy.26 = f32[1024,128]{0,1:T(8,128)S(1)} copy(f32[1024,128]{1,0:T(8,128)} %scatter_custom_fusion) | data formatting | bytes 1048576 | tf_op jit(solution)/shard_map/scatter | solution.py:23
  21.6 0.0 copy-done.2
  21.6 0.0 copy-done.3
  21.6 0.0 copy-done.4
  21.6 0.6 fusion.13
  22.2 0.0 copy-start.5
  22.2 26.5 %all-gather = bf16[8,6,128]{2,1,0:T(8,128)(2,1)S(1)} all-gather(bf16[1,6,128]{2,1,0:T(8,128)(2,1)S(1)} %fusion.13), channel_id=1, replica_groups=mesh['gx'=4,'gy'=8] {'gy'}, dimensions={0}, use_global_device_ids=true | all-gather | bytes 13824 | tf_op jit(solution)/shard_map/all_gather | solution.py:28
  48.7 6.5 %all_gather.7 = bf16[192,128]{1,0:T(8,128)(2,1)S(1)} all-gather(bf16[48,128]{1,0:T(8,128)(2,1)S(1)} %reshape.66), channel_id=1, replica_groups=mesh['gx'=4,'gy'=8] {'gx'}, dimensions={0}, use_global_device_ids=true | all-gather | bytes 61440 | tf_op jit(solution)/shard_map/all_gather | solution.py:31
  55.2 0.0 copy-done
  55.2 0.8 %fusion.10 = f32[1024,128]{0,1:T(8,128)S(1)} fusion(bf16[1,1,1024,1024]{3,2,1,0:T(8,128)(2,1)S(1)} %copy-done, f32[1,1,1024,128]{2,3,1,0:T(8,128)S(1)} %copy.23, f32[1024,128]{0,1:T(8,128)S(1)} %copy.26, bf16[1,1,1024,128]{2,3,1,0:T(8,128)(2,1)S(1)} %copy.24, f32[1024]{0:T(1024)S(1)} %bitcast.60, f32[1024]{0:T(1024)S(1)} %bitcast.62, f32[1024]{0:T(1024)S(1)} %bitcast.63), kind=kOutput, calls=%fused_computation.9 | convolution fusion | flops 269484032 | bytes 3944448 | tf_op jit(solution)/shard_map/dot_general | solution.py:57
  56.0 0.0 copy-done.5
  56.0 0.1 fusion.32
  56.1 0.7 %fusion.3 = f32[1,1,1024,128]{2,3,1,0:T(8,128)S(1)} fusion(f32[1024,128]{0,1:T(8,128)S(1)} %fusion.10, f32[128,6]{0,1:T(8,128)S(1)} %fusion.32, f32[1,1,1024,6]{2,1,3,0:T(1,128)S(1)} %copy-done.2), kind=kOutput, calls=%fused_computation.6 | convolution fusion | flops 9568256 | bytes 1076224 | tf_op jit(solution)/shard_map/dot_general | solution.py:62
  56.8 1.0 %copy.27 = f32[1,1,1024,128]{3,2,1,0:T(8,128)} copy(f32[1,1,1024,128]{2,3,1,0:T(8,128)S(1)} %fusion.3) | data formatting | bytes 1048576 | tf_op jit(solution)/shard_map/broadcast_in_dim | solution.py:64
  (3 shorter events, 0.0 us)
Async XLA Ops:
  0.0 55.2 %copy-start = (bf16[1,1,1024,1024]{3,2,1,0:T(8,128)(2,1)S(1)}, bf16[1,1,1024,1024]{3,2,1,0:T(8,128)(2,1)}, u32[]{:S(2)}) copy-start(bf16[1,1,1024,1024]{3,2,1,0:T(8,128)(2,1)} %param.11) | copy-start | bytes 6291460
  0.0 16.1 %copy-start.1 = (f32[1,1,1024,128]{3,2,1,0:T(8,128)S(1)}, f32[1,1,1024,128]{3,2,1,0:T(8,128)}, u32[]{:S(2)}) copy-start(f32[1,1,1024,128]{3,2,1,0:T(8,128)} %param.10) | copy-start | bytes 1572868
  0.9 16.5 %copy-start.6 = (s32[1,1,1024]{2,1,0:T(1,128)S(1)}, s32[1,1,1024]{2,1,0:T(1,128)}, u32[]{:S(2)}) copy-start(s32[1,1,1024]{2,1,0:T(1,128)} %param.15) | copy-start | bytes 12292
  3.0 18.6 %copy-start.2 = (f32[1,1,1024,6]{2,1,3,0:T(1,128)S(1)}, f32[1,1,1024,6]{2,1,3,0:T(1,128)}, u32[]{:S(2)}) copy-start(f32[1,1,1024,6]{2,1,3,0:T(1,128)} %param.16) | copy-start | bytes 73732
  3.0 18.6 %copy-start.3 = (f32[1,1,1024]{2,1,0:T(1,128)S(1)}, f32[1,1,1024]{2,1,0:T(1,128)}, u32[]{:S(2)}) copy-start(f32[1,1,1024]{2,1,0:T(1,128)} %param.13) | copy-start | bytes 12292
  3.0 18.6 %copy-start.4 = (f32[1,1,1024]{2,1,0:T(1,128)S(1)}, f32[1,1,1024]{2,1,0:T(1,128)}, u32[]{:S(2)}) copy-start(f32[1,1,1024]{2,1,0:T(1,128)} %param.12) | copy-start | bytes 12292
  3.7 13.7 %collective-permute-start.3 = (f32[128,128]{1,0:T(8,128)}, f32[128,128]{1,0:T(8,128)S(1)}, u32[]{:S(2)}, u32[]{:S(2)}) collective-permute-start(f32[128,128]{1,0:T(8,128)} %get-tuple-element.8), channel_id=1, source_target_pairs={{1,0},{2,1},{3,2},{4,3},{5,4},{6,5},{7,6},{9,8},{10,9},{11,10},{12... | collective-permute-start | bytes 196616 | tf_op jit(solution)/shard_map/ppermute | solution.py:12
  5.0 12.4 %collective-permute-start.2 = (f32[128,128]{1,0:T(8,128)}, f32[128,128]{1,0:T(8,128)}, u32[]{:S(2)}, u32[]{:S(2)}) collective-permute-start(f32[128,128]{1,0:T(8,128)} %get-tuple-element.6), channel_id=1, source_target_pairs={{0,1},{1,2},{2,3},{3,4},{4,5},{5,6},{6,7},{8,9},{9,10},{10,11},{11... | collective-permute-start | bytes 196616 | tf_op jit(solution)/shard_map/ppermute | solution.py:12
  11.1 6.3 %collective-permute-start.1 = (f32[128,128]{1,0:T(8,128)}, f32[128,128]{1,0:T(8,128)}, u32[]{:S(2)}, u32[]{:S(2)}) collective-permute-start(f32[128,128]{1,0:T(8,128)} %get-tuple-element.7), channel_id=1, source_target_pairs={{8,0},{16,8},{24,16},{9,1},{17,9},{25,17},{10,2},{18,10},{26,18},{... | collective-permute-start | bytes 196616 | tf_op jit(solution)/shard_map/ppermute | solution.py:12
  12.4 5.0 %collective-permute-start = (f32[128,128]{1,0:T(8,128)}, f32[128,128]{1,0:T(8,128)}, u32[]{:S(2)}, u32[]{:S(2)}) collective-permute-start(f32[128,128]{1,0:T(8,128)} %get-tuple-element.5), channel_id=1, source_target_pairs={{0,8},{8,16},{16,24},{1,9},{9,17},{17,25},{2,10},{10,18},{18,26},{... | collective-permute-start | bytes 196616 | tf_op jit(solution)/shard_map/ppermute | solution.py:12
  22.2 33.8 %copy-start.5 = (bf16[6,192]{1,0:T(8,128)(2,1)S(1)}, bf16[6,192]{1,0:T(8,128)(2,1)}, u32[]{:S(2)}) copy-start(bf16[6,192]{1,0:T(8,128)(2,1)} %param.17) | copy-start | bytes 6916
where the time goes:
time: 58.2 us; the launch traced here: 57.8 us
  blocking collectives  33 us (57%)
  starting transfers between devices  12.4 us (21%)
  local copies, waits for them, and re-layouts  6.34 us (11%)
  other arithmetic  3.71 us (6%)
  matrix products  2.19 us (4%)
    all_gather x1, blocking collectives, coarse_solve(): grid_row = lax.all_gather(coarse_res, 'gy', axis=0, tiled=True)  26.5 us
    ppermute x4, starting transfers between devices, shifted(): return lax.ppermute(shard, axis, pairs)  12.4 us
    all_gather x1, blocking collectives, coarse_solve(): lax.all_gather(grid_row, 'gx', axis=0, tiled=True)  6.5 us
    scatter x1, other arithmetic, apply_operator(): placed = jnp.zeros(field.shape, jnp.float32).at[side_order].set(received)  2.86 us
    gather x1, local copies, waits for them, and re-layouts, apply_operator(): interface_values = field[side_order].reshape(4, IR, field.shape[1])  2.08 us
    unnamed x17, local copies, waits for them, and re-layouts  1.33 us
    scatter x1, local copies, waits for them, and re-layouts, apply_operator(): placed = jnp.zeros(field.shape, jnp.float32).at[side_order].set(received)  1.24 us
  transfers between devices with their start and end apart: 4, of which 0 were waited for; matrix products, arithmetic and copies ran while one was open for 2% of the time, Pallas kernels for 0%

commit v1 on v0

v1 whole, which is shorter than its diff:
```python
import functools

import jax
import jax.numpy as jnp
from jax import lax
from jax.experimental import pallas as pl
from jax.experimental.pallas import tpu as pltpu
from jax.sharding import PartitionSpec as P

MESH = pl.DeviceIdType.MESH
LANES = 128
SLOT = 8


def one_hot(mask):
    return jnp.where(mask, 1.0, 0.0).astype(jnp.bfloat16)


def split(values):
    high = values.astype(jnp.bfloat16)
    return high, (values - high.astype(jnp.float32)).astype(jnp.bfloat16)


def peer_offsets(nx, ny):
    offsets = [(a, b) for a in range(nx) for b in range(ny) if a or b]
    return sorted(offsets, key=lambda o: abs(o[1] - ny // 2))


def for_each_peer(nx, ny, ix, iy, action):
    if nx * ny <= 64:
        for a, b in peer_offsets(nx, ny):
            action(lax.rem(ix + a, nx), lax.rem(iy + b, ny))
        return

    def step(offset, carry):
        action(lax.rem(ix + offset // ny, nx), lax.rem(iy + offset % ny, ny))
        return carry

    lax.fori_loop(1, nx * ny, step, 0)


def kernel(
    nx, ny, modes_count,
    loads_h, guess_h, inverse_h, diag_h, coup_h, rows_h, owned_h, modes_h, cinv_h,
    out_h,
    loads, guess, inverse, diag, coup, rows, owned, modes, cinv,
    halo_send, halo_recv, place, base, total, gathered, coarse_send, spread, lift,
    in_sem, halo_ssem, halo_rsem, coarse_ssem, coarse_rsem, out_sem,
):
    n = nx * ny
    m, k = guess.shape
    chunks = m // LANES
    ix, iy = lax.axis_index("gx"), lax.axis_index("gy")
    me = ix * ny + iy

    pairs = [
        (rows_h, rows), (guess_h, guess), (coup_h, coup), (modes_h, modes),
        (diag_h, diag), (loads_h, loads), (cinv_h, cinv), (owned_h, owned),
        (inverse_h, inverse),
    ]
    fetch = [pltpu.make_async_copy(a, b, in_sem.at[i]) for i, (a, b) in enumerate(pairs)]
    for copy in fetch:
        copy.start()
    barrier = pltpu.get_barrier_semaphore()
    for_each_peer(
        nx, ny, ix, iy,
        lambda px, py: pl.semaphore_signal(barrier, inc=1, device_id=(px, py), device_id_type=MESH),
    )

    fetch[0].wait()
    fetch[1].wait()
    guess_half = guess[...].astype(jnp.bfloat16)
    row_columns = rows[...].astype(jnp.float32).T
    lane = lax.broadcasted_iota(jnp.int32, (LANES, m), 1).astype(jnp.float32)
    for side in range(4):
        pick = one_hot(lane == row_columns[:, side : side + 1])
        values = jnp.dot(pick, guess_half, preferred_element_type=jnp.float32)
        halo_send[side] = values.astype(jnp.bfloat16)
    for side, edge in enumerate((ix == 0, ix == nx - 1, iy == 0, iy == ny - 1)):
        @pl.when(edge)
        def _():
            halo_recv[side] = jnp.zeros((LANES, k), jnp.bfloat16)

    pl.semaphore_wait(barrier, n - 1)

    sends = []
    for source, target, exists, dx, dy in (
        (3, 2, iy < ny - 1, 0, 1),
        (2, 3, iy > 0, 0, -1),
        (1, 0, ix < nx - 1, 1, 0),
        (0, 1, ix > 0, -1, 0),
    ):
        copy = pltpu.make_async_remote_copy(
            src_ref=halo_send.at[source],
            dst_ref=halo_recv.at[target],
            send_sem=halo_ssem.at[source],
            recv_sem=halo_rsem.at[target],
            device_id=(ix + dx, iy + dy),
            device_id_type=MESH,
        )
        sends.append((copy, exists))
        pl.when(exists)(copy.start)

    row_lanes = jnp.concatenate([rows[s : s + 1, :] for s in range(4)], axis=1)
    for j in range(chunks):
        sub = lax.broadcasted_iota(jnp.int32, (LANES, 4 * LANES), 0) + j * LANES
        place[j * LANES : (j + 1) * LANES, :] = one_hot(sub == row_lanes)
    fetch[2].wait()
    fetch[3].wait()
    zero_rows = jnp.zeros((SLOT - modes_count, LANES), jnp.float32)
    mode_rows = [
        jnp.concatenate([modes[c, :, j * LANES : (j + 1) * LANES] for c in range(modes_count)] + [zero_rows], axis=0)
        for j in range(chunks)
    ]
    scaled = jnp.concatenate([mode_rows[j] * coup[j : j + 1, :] for j in range(chunks)], axis=1)
    scaled = jnp.concatenate(split(scaled), axis=0)
    coarse_pick = jnp.dot(scaled, place[...], preferred_element_type=jnp.float32).astype(jnp.bfloat16)

    fetch[4].wait()
    fetch[5].wait()
    diag_columns = diag[...].T
    for j in range(chunks):
        at = pl.ds(j * LANES, LANES)
        base[at, :] = loads[at, :].astype(jnp.float32) - diag_columns[:, j : j + 1] * guess[at, :]
    coarse_base = jnp.dot(
        jnp.concatenate(mode_rows, axis=1), base[...],
        precision=lax.Precision.HIGHEST, preferred_element_type=jnp.float32,
    )

    fetch[6].wait()
    group = min(n, 64)
    narrow, wide = group * modes_count, group * SLOT
    wide_at = lax.broadcasted_iota(jnp.int32, (narrow, wide), 1)
    slot_row = lax.rem(wide_at, SLOT)
    source_row = lax.div(wide_at, SLOT) * modes_count + slot_row
    narrow_at = lax.broadcasted_iota(jnp.int32, (narrow, wide), 0)
    expand = one_hot((narrow_at == source_row) & (slot_row < modes_count))
    for g in range(n // group):
        spread[:, g * wide : (g + 1) * wide] = jnp.dot(
            cinv[:, g * narrow : (g + 1) * narrow], expand, preferred_element_type=jnp.float32
        ).astype(jnp.bfloat16)
    for j in range(chunks):
        high, low = split(mode_rows[j])
        high, low = high.astype(jnp.float32), low.astype(jnp.float32)
        stack = jnp.concatenate(
            [high, high, low, jnp.zeros((LANES - 3 * SLOT, LANES), jnp.float32)], axis=0
        )
        lift[j * LANES : (j + 1) * LANES, :] = stack.T.astype(jnp.bfloat16)

    for copy, exists in sends:
        pl.when(exists)(copy.wait_send)
    for side, exists in enumerate((ix > 0, ix < nx - 1, iy > 0, iy < ny - 1)):
        slot = halo_recv.at[side]
        arrival = pltpu.make_async_copy(slot, slot, halo_rsem.at[side])
        pl.when(exists)(arrival.wait)

    received = halo_recv[...].reshape(4 * LANES, k)
    terms = jnp.dot(coarse_pick, received, preferred_element_type=jnp.float32)
    coarse = (coarse_base + terms[:SLOT] + terms[SLOT:]).astype(jnp.bfloat16)
    coarse_send[...] = coarse
    gathered[pl.ds(me, 1)] = coarse[None]

    def send_coarse(px, py):
        pltpu.make_async_remote_copy(
            src_ref=coarse_send,
            dst_ref=gathered.at[me],
            send_sem=coarse_ssem,
            recv_sem=coarse_rsem,
            device_id=(px, py),
            device_id_type=MESH,
        ).start()

    for_each_peer(nx, ny, ix, iy, send_coarse)

    coup_columns = coup[...].T
    placed = jnp.dot(place[...], received, preferred_element_type=jnp.float32)
    residual_half = []
    for j in range(chunks):
        at = slice(j * LANES, (j + 1) * LANES)
        residual_half.append(
            (base[at, :] + coup_columns[:, j : j + 1] * placed[at]).astype(jnp.bfloat16)
        )
    residual_half = jnp.concatenate(residual_half, axis=0)
    fetch[7].wait()
    fetch[8].wait()
    owned_columns = owned[...].astype(jnp.float32).T
    for j in range(chunks):
        at = slice(j * LANES, (j + 1) * LANES)
        local = jnp.dot(inverse[at, :], residual_half, preferred_element_type=jnp.float32)
        total[at, :] = guess[at, :] + owned_columns[:, j : j + 1] * local

    everyone = gathered.at[pl.ds(0, n - 1)]
    pltpu.make_async_copy(everyone, everyone, coarse_ssem).wait()
    pltpu.make_async_copy(everyone, everyone, coarse_rsem).wait()

    coef = jnp.dot(
        spread[...], gathered[...].reshape(n * SLOT, k), preferred_element_type=jnp.float32
    )
    coef = jnp.concatenate([coef, jnp.zeros((SLOT - modes_count, k), jnp.float32)], axis=0)
    high, low = split(coef)
    stack = jnp.concatenate(
        [high, low, high, jnp.zeros((LANES - 3 * SLOT, k), jnp.bfloat16)], axis=0
    )
    stores = []
    for j in range(chunks):
        at = pl.ds(j * LANES, LANES)
        total[at, :] = total[at, :] + jnp.dot(
            lift[at, :], stack, preferred_element_type=jnp.float32
        )
        copy = pltpu.make_async_copy(total.at[at], out_h.at[at], out_sem.at[j])
        copy.start()
        stores.append(copy)
    for copy in stores:
        copy.wait()


def body(nx, ny, *args):
    loads, guess, inverse, diag, coup, rows, owned, modes, cinv = args
    m, k = guess.shape[2:]
    modes_count = modes.shape[3]
    n = nx * ny
    chunks = m // LANES
    small = (chunks, LANES)
    operands = (
        loads[0, 0], guess[0, 0], inverse[0, 0],
        diag.reshape(small), coup.reshape(small), rows.reshape(small), owned.reshape(small),
        jnp.transpose(modes[0], (2, 0, 1)), cinv,
    )
    scratch = [pltpu.VMEM(a.shape, a.dtype) for a in operands] + [
        pltpu.VMEM((4, LANES, k), jnp.bfloat16),
        pltpu.VMEM((4, LANES, k), jnp.bfloat16),
        pltpu.VMEM((m, 4 * LANES), jnp.bfloat16),
        pltpu.VMEM((m, k), jnp.float32),
        pltpu.VMEM((m, k), jnp.float32),
        pltpu.VMEM((n, SLOT, k), jnp.bfloat16),
        pltpu.VMEM((SLOT, k), jnp.bfloat16),
        pltpu.VMEM((modes_count, n * SLOT), jnp.bfloat16),
        pltpu.VMEM((m, LANES), jnp.bfloat16),
        pltpu.SemaphoreType.DMA((len(operands),)),
        pltpu.SemaphoreType.DMA((4,)),
        pltpu.SemaphoreType.DMA((4,)),
        pltpu.SemaphoreType.DMA,
        pltpu.SemaphoreType.DMA,
        pltpu.SemaphoreType.DMA((chunks,)),
    ]
    result = pl.pallas_call(
        functools.partial(kernel, nx, ny, modes_count),
        out_shape=jax.ShapeDtypeStruct((m, k), jnp.float32),
        in_specs=[pl.BlockSpec(memory_space=pl.ANY)] * len(operands),
        out_specs=pl.BlockSpec(memory_space=pl.ANY),
        scratch_shapes=scratch,
        compiler_params=pltpu.CompilerParams(collective_id=0, has_side_effects=True),
    )(*operands)
    return result[None, None]


def solution(mesh):
    nx, ny = mesh.shape["gx"], mesh.shape["gy"]
    return jax.shard_map(
        functools.partial(body, nx, ny),
        mesh=mesh,
        in_specs=(
            P("gx", "gy", None, None),
            P("gx", "gy", None, None),
            P("gx", "gy", None, None),
            P("gx", "gy", None),
            P("gx", "gy", None),
            P("gx", "gy", None),
            P("gx", "gy", None),
            P("gx", "gy", None, None),
            P(("gx", "gy"), None),
        ),
        out_specs=P("gx", "gy", None, None),
        check_vma=False,
    )
```

time: 58.2 us -> 17.1 us (0.29)
  blocking collectives: 33 us -> 0 us
  Pallas kernels: 0 us -> 15 us
  starting transfers between devices: 12.4 us -> 0 us
  local copies, waits for them, and re-layouts: 6.34 us -> 1.87 us
  other arithmetic: 3.71 us -> 0 us
  matrix products: 2.19 us -> 0 us
    all_gather x2 -> x0, blocking collectives: 33 us -> none  [the longest x1 26.5 us: coarse_solve(): grid_row = lax.all_gather(coarse_res, 'gy', axis=0, tiled=True)]
    pallas_call x0 -> x1, Pallas kernels: none -> 15 us  [body(): pl.pallas_call(functools.partial(kernel, nx, ny, modes_count), out_shape=...]
    ppermute x4 -> x0, starting transfers between devices: 12.4 us -> none  [shifted(): return lax.ppermute(shard, axis, pairs)]
    scatter x1 -> x0, other arithmetic: 2.86 us -> none  [apply_operator(): placed = jnp.zeros(field.shape, jnp.float32).at[side_order].set(received)]
    dot_general x4 -> x0, matrix products: 2.19 us -> none  [the longest x1 0.83 us: body(): jnp.dot(inverse, residual_half, preferred_element_type=jnp.float32)]
    gather x1 -> x0, local copies, waits for them, and re-layouts: 2.08 us -> none  [apply_operator(): interface_values = field[side_order].reshape(4, IR, field.shape[1])]
    scatter x1 -> x0, local copies, waits for them, and re-layouts: 1.24 us -> none  [apply_operator(): placed = jnp.zeros(field.shape, jnp.float32).at[side_order].set(received)]
    broadcast_in_dim x1 -> x0, local copies, waits for them, and re-layouts: 1 us -> none  [body(): return solution[None, None]]
  transfers between devices with their start and end apart: 4 -> 0, of which waited for: 0 -> 0; matrix products, arithmetic and copies ran while one was open for 2% -> 0% of each run, Pallas kernels for 0% -> 0%
where the time goes in v1:
time: 17.1 us; the launch traced here: 16.9 us
  Pallas kernels  15 us (88%)
  local copies, waits for them, and re-layouts  1.87 us (11%)
    pallas_call x1, Pallas kernels, body(): pl.pallas_call(functools.partial(kernel, nx, ny, modes_count), out_shape=...  15 us
    unnamed x1, local copies, waits for them, and re-layouts  1.87 us

profile of v1, /device:TPU:0, one launch (start us, length us, event | category | flops | bytes accessed | tf_op | source)
XLA Modules:
  0.0 16.9 jit_solution(9827588425419891429)
XLA Ops:
  0.0 15.0 %shard_map.91 = f32[1024,128]{1,0:T(8,128)} custom-call(bf16[1024,128]{1,0:T(8,128)(2,1)} %bitcast.14, f32[1024,128]{1,0:T(8,128)} %bitcast.13, bf16[1024,1024]{1,0:T(8,128)(2,1)} %bitcast.11, f32[8,128]{1,0:T(8,128)} %bitcast.16, f32[8,128]{1,0:T(8,128)} %bitcast.17, s32[8,128]{1,0:T(8,128)} %bitcast.18, s32[8,128]{1,0:T(8,128)} %bitcast.19, ...), custom_call_target="tpu_custom_call" | custom-call | tf_op jit(solution)/shard_map/pallas_call | solution.py:246
  15.0 1.9 %copy.11 = f32[1,1,1024,128]{3,2,1,0:T(8,128)} copy(f32[1,1,1024,128]{3,2,1,0:T(8,128)} %bitcast.12) | data formatting | bytes 1048576

commit v2 on v1

--- a/solution.py
+++ b/solution.py
@@ -39,13 +39,38 @@
     lax.fori_loop(1, nx * ny, step, 0)
 
 
+def column_reaches(ny):
+    reaches = [2]
+    while 2 * reaches[-1] < ny - 1:
+        reaches.append(2 * reaches[-1])
+    return reaches
+
+
+def greet_column(ny, ix, iy, semaphore, reach):
+    for step in (reach, -reach):
+        there = iy + step
+
+        @pl.when((there >= 0) & (there < ny))
+        def _():
+            pl.semaphore_signal(semaphore, inc=1, device_id=(ix, there), device_id_type=MESH)
+
+    return jnp.where(iy + reach < ny, 1, 0) + jnp.where(iy >= reach, 1, 0)
+
+
+def greet_row(nx, ix, iy, semaphore):
+    for step in range(1, nx):
+        there = lax.rem(ix + step, nx)
+        pl.semaphore_signal(semaphore, inc=1, device_id=(there, iy), device_id_type=MESH)
+    return nx - 1
+
+
 def kernel(
     nx, ny, modes_count,
     loads_h, guess_h, inverse_h, diag_h, coup_h, rows_h, owned_h, modes_h, cinv_h,
     out_h,
     loads, guess, inverse, diag, coup, rows, owned, modes, cinv,
     halo_send, halo_recv, place, base, total, gathered, coarse_send, spread, lift,
-    in_sem, halo_ssem, halo_rsem, coarse_ssem, coarse_rsem, out_sem,
+    in_sem, halo_ssem, halo_rsem, coarse_ssem, coarse_rsem, out_sem, ready,
 ):
     n = nx * ny
     m, k = guess.shape
@@ -62,10 +87,8 @@
     for copy in fetch:
         copy.start()
     barrier = pltpu.get_barrier_semaphore()
-    for_each_peer(
-        nx, ny, ix, iy,
-        lambda px, py: pl.semaphore_signal(barrier, inc=1, device_id=(px, py), device_id_type=MESH),
-    )
+    greeted = greet_row(nx, ix, iy, barrier)
+    greeted += greet_column(ny, ix, iy, barrier, 1) + greet_column(ny, ix, iy, barrier, 2)
 
     fetch[0].wait()
     fetch[1].wait()
@@ -81,7 +104,7 @@
         def _():
             halo_recv[side] = jnp.zeros((LANES, k), jnp.bfloat16)
 
-    pl.semaphore_wait(barrier, n - 1)
+    pl.semaphore_wait(barrier, greeted)
 
     sends = []
     for source, target, exists, dx, dy in (
@@ -100,6 +123,8 @@
         )
         sends.append((copy, exists))
         pl.when(exists)(copy.start)
+    reaches = column_reaches(ny)
+    expected = greet_column(ny, ix, iy, ready.at[0], reaches[0])
 
     row_lanes = jnp.concatenate([rows[s : s + 1, :] for s in range(4)], axis=1)
     for j in range(chunks):
@@ -116,12 +141,21 @@
     scaled = jnp.concatenate(split(scaled), axis=0)
     coarse_pick = jnp.dot(scaled, place[...], preferred_element_type=jnp.float32).astype(jnp.bfloat16)
 
-    fetch[4].wait()
-    fetch[5].wait()
-    diag_columns = diag[...].T
-    for j in range(chunks):
-        at = pl.ds(j * LANES, LANES)
-        base[at, :] = loads[at, :].astype(jnp.float32) - diag_columns[:, j : j + 1] * guess[at, :]
+    def late_base():
+        fetch[4].wait()
+        fetch[5].wait()
+        diag_columns = diag[...].T
+        for j in range(chunks):
+            at = pl.ds(j * LANES, LANES)
+            base[at, :] = loads[at, :].astype(jnp.float32) - diag_columns[:, j : j + 1] * guess[at, :]
+
+    for step, reach in enumerate(reaches):
+        pl.semaphore_wait(ready.at[step], expected)
+        if step + 1 < len(reaches):
+            expected = greet_column(ny, ix, iy, ready.at[step + 1], reaches[step + 1])
+        if step == 0:
+            late_base()
+    expected = greet_row(nx, ix, iy, ready.at[len(reaches)])
     coarse_base = jnp.dot(
         jnp.concatenate(mode_rows, axis=1), base[...],
         precision=lax.Precision.HIGHEST, preferred_element_type=jnp.float32,
@@ -147,8 +181,7 @@
         )
         lift[j * LANES : (j + 1) * LANES, :] = stack.T.astype(jnp.bfloat16)
 
-    for copy, exists in sends:
-        pl.when(exists)(copy.wait_send)
+    pl.semaphore_wait(ready.at[len(reaches)], expected)
     for side, exists in enumerate((ix > 0, ix < nx - 1, iy > 0, iy < ny - 1)):
         slot = halo_recv.at[side]
         arrival = pltpu.make_async_copy(slot, slot, halo_rsem.at[side])
@@ -189,6 +222,8 @@
         local = jnp.dot(inverse[at, :], residual_half, preferred_element_type=jnp.float32)
         total[at, :] = guess[at, :] + owned_columns[:, j : j + 1] * local
 
+    for copy, exists in sends:
+        pl.when(exists)(copy.wait_send)
     everyone = gathered.at[pl.ds(0, n - 1)]
     pltpu.make_async_copy(everyone, everyone, coarse_ssem).wait()
     pltpu.make_async_copy(everyone, everyone, coarse_rsem).wait()
@@ -242,6 +277,7 @@
         pltpu.SemaphoreType.DMA,
         pltpu.SemaphoreType.DMA,
         pltpu.SemaphoreType.DMA((chunks,)),
+        pltpu.SemaphoreType.REGULAR((len(column_reaches(ny)) + 1,)),
     ]
     result = pl.pallas_call(
         functools.partial(kernel, nx, ny, modes_count),

time: 17.1 us -> 16.9 us (0.988)
  no operation moved by 1% of the time
where the time goes in v2:
time: 16.9 us; the launch traced here: 16.8 us
  Pallas kernels  14.9 us (88%)
  local copies, waits for them, and re-layouts  1.87 us (11%)
    pallas_call x1, Pallas kernels, body(): pl.pallas_call(functools.partial(kernel, nx, ny, modes_count), out_shape=...  14.9 us
    unnamed x1, local copies, waits for them, and re-layouts  1.87 us

profile of v2, /device:TPU:0, one launch (start us, length us, event | category | flops | bytes accessed | tf_op | source)
XLA Modules:
  0.0 16.8 jit_solution(6546497891643586625)
XLA Ops:
  0.0 14.9 %shard_map.91 = f32[1024,128]{1,0:T(8,128)} custom-call(bf16[1024,128]{1,0:T(8,128)(2,1)} %bitcast.14, f32[1024,128]{1,0:T(8,128)} %bitcast.13, bf16[1024,1024]{1,0:T(8,128)(2,1)} %bitcast.11, f32[8,128]{1,0:T(8,128)} %bitcast.16, f32[8,128]{1,0:T(8,128)} %bitcast.17, s32[8,128]{1,0:T(8,128)} %bitcast.18, s32[8,128]{1,0:T(8,128)} %bitcast.19, ...), custom_call_target="tpu_custom_call" | custom-call | tf_op jit(solution)/shard_map/pallas_call | solution.py:282
  14.9 1.9 %copy.11 = f32[1,1,1024,128]{3,2,1,0:T(8,128)} copy(f32[1,1,1024,128]{3,2,1,0:T(8,128)} %bitcast.12) | data formatting | bytes 1048576

commit v3 on v2

--- a/solution.py
+++ b/solution.py
@@ -67,10 +67,10 @@
 def kernel(
     nx, ny, modes_count,
     loads_h, guess_h, inverse_h, diag_h, coup_h, rows_h, owned_h, modes_h, cinv_h,
-    out_h,
+    total, lift, stack_out,
     loads, guess, inverse, diag, coup, rows, owned, modes, cinv,
-    halo_send, halo_recv, place, base, total, gathered, coarse_send, spread, lift,
-    in_sem, halo_ssem, halo_rsem, coarse_ssem, coarse_rsem, out_sem, ready,
+    halo_send, halo_recv, place, base, gathered, coarse_send, spread,
+    in_sem, halo_ssem, halo_rsem, coarse_ssem, coarse_rsem, ready,
 ):
     n = nx * ny
     m, k = guess.shape
@@ -233,16 +233,20 @@
     )
     coef = jnp.concatenate([coef, jnp.zeros((SLOT - modes_count, k), jnp.float32)], axis=0)
     high, low = split(coef)
-    stack = jnp.concatenate(
+    stack_out[...] = jnp.concatenate(
         [high, low, high, jnp.zeros((LANES - 3 * SLOT, k), jnp.bfloat16)], axis=0
     )
+
+
+def finish(total, lift, stack, out_h, staged, out_sem):
+    chunks = total.shape[0] // LANES
     stores = []
     for j in range(chunks):
         at = pl.ds(j * LANES, LANES)
-        total[at, :] = total[at, :] + jnp.dot(
-            lift[at, :], stack, preferred_element_type=jnp.float32
+        staged[at, :] = total[at, :] + jnp.dot(
+            lift[at, :], stack[...], preferred_element_type=jnp.float32
         )
-        copy = pltpu.make_async_copy(total.at[at], out_h.at[at], out_sem.at[j])
+        copy = pltpu.make_async_copy(staged.at[at], out_h.at[at], out_sem.at[j])
         copy.start()
         stores.append(copy)
     for copy in stores:
@@ -266,27 +270,40 @@
         pltpu.VMEM((4, LANES, k), jnp.bfloat16),
         pltpu.VMEM((m, 4 * LANES), jnp.bfloat16),
         pltpu.VMEM((m, k), jnp.float32),
-        pltpu.VMEM((m, k), jnp.float32),
         pltpu.VMEM((n, SLOT, k), jnp.bfloat16),
         pltpu.VMEM((SLOT, k), jnp.bfloat16),
         pltpu.VMEM((modes_count, n * SLOT), jnp.bfloat16),
-        pltpu.VMEM((m, LANES), jnp.bfloat16),
         pltpu.SemaphoreType.DMA((len(operands),)),
         pltpu.SemaphoreType.DMA((4,)),
         pltpu.SemaphoreType.DMA((4,)),
         pltpu.SemaphoreType.DMA,
         pltpu.SemaphoreType.DMA,
-        pltpu.SemaphoreType.DMA((chunks,)),
         pltpu.SemaphoreType.REGULAR((len(column_reaches(ny)) + 1,)),
     ]
+    vmem = pl.BlockSpec(memory_space=pltpu.VMEM)
+    anywhere = pl.BlockSpec(memory_space=pl.ANY)
+    parts = pl.pallas_call(
+        functools.partial(kernel, nx, ny, modes_count),
+        out_shape=(
+            pltpu.VMEM((m, k), jnp.float32),
+            pltpu.VMEM((m, LANES), jnp.bfloat16),
+            pltpu.VMEM((LANES, k), jnp.bfloat16),
+        ),
+        in_specs=[pl.BlockSpec(memory_space=pltpu.HBM)] * len(operands),
+        out_specs=[vmem] * 3,
+        scratch_shapes=scratch,
+        compiler_params=pltpu.CompilerParams(
+            collective_id=0, has_side_effects=True, vmem_limit_bytes=40 << 20
+        ),
+    )(*operands)
     result = pl.pallas_call(
-        functools.partial(kernel, nx, ny, modes_count),
+        finish,
         out_shape=jax.ShapeDtypeStruct((m, k), jnp.float32),
-        in_specs=[pl.BlockSpec(memory_space=pl.ANY)] * len(operands),
-        out_specs=pl.BlockSpec(memory_space=pl.ANY),
-        scratch_shapes=scratch,
-        compiler_params=pltpu.CompilerParams(collective_id=0, has_side_effects=True),
-    )(*operands)
+        in_specs=[vmem] * 3,
+        out_specs=anywhere,
+        scratch_shapes=[pltpu.VMEM((m, k), jnp.float32), pltpu.SemaphoreType.DMA((chunks,))],
+        compiler_params=pltpu.CompilerParams(vmem_limit_bytes=16 << 20),
+    )(*parts)
     return result[None, None]
 
 

time: 16.9 us -> 23.3 us (1.38); the launches traced: 16.8 us -> 22.8 us
  local copies, waits for them, and re-layouts: 1.87 us -> 7.75 us
    unnamed x1 -> x18, local copies, waits for them, and re-layouts: 1.87 us -> 7.75 us
    pallas_call x0 -> x1, Pallas kernels: none -> 1.01 us  [body(): pl.pallas_call(finish, out_shape=jax.ShapeDtypeStruct((m, k), jnp.float32...]
    pallas_call x1, Pallas kernels: 14.9 us -> 14 us  [body(): pl.pallas_call(functools.partial(kernel, nx, ny, modes_count), out_shape=...]
where the time goes in v3:
time: 23.3 us; the launch traced here: 22.8 us
  Pallas kernels  15 us (64%)
  local copies, waits for them, and re-layouts  7.75 us (33%)
    pallas_call x1, Pallas kernels, body(): pl.pallas_call(functools.partial(kernel, nx, ny, modes_count), out_shape=...  14 us
    unnamed x18, local copies, waits for them, and re-layouts  7.75 us
    pallas_call x1, Pallas kernels, body(): pl.pallas_call(finish, out_shape=jax.ShapeDtypeStruct((m, k), jnp.float32...  1.01 us

profile of v3, /device:TPU:0, one launch (start us, length us, event | category | flops | bytes accessed | tf_op | source)
XLA Modules:
  0.0 22.8 jit_solution(12318418146222091572)
XLA Ops:
  0.0 0.0 copy-start
  0.0 1.6 %copy-done = bf16[1,1,1024,1024]{3,2,1,0:T(8,128)(2,1)S(1)} copy-done((bf16[1,1,1024,1024]{3,2,1,0:T(8,128)(2,1)S(1)}, bf16[1,1,1024,1024]{3,2,1,0:T(8,128)(2,1)}, u32[]{:S(2)}) %copy-start) | copy-done | bytes 2097176
  1.6 0.0 copy-start.1
  1.6 1.0 %copy-done.1 = f32[1,1,1024,128]{3,2,1,0:T(8,128)S(1)} copy-done((f32[1,1,1024,128]{3,2,1,0:T(8,128)S(1)}, f32[1,1,1024,128]{3,2,1,0:T(8,128)}, u32[]{:S(2)}) %copy-start.1) | copy-done | bytes 524312
  2.6 0.0 copy-start.2
  2.6 0.9 %copy-done.2 = bf16[1,1,1024,128]{3,2,1,0:T(8,128)(2,1)S(1)} copy-done((bf16[1,1,1024,128]{3,2,1,0:T(8,128)(2,1)S(1)}, bf16[1,1,1024,128]{3,2,1,0:T(8,128)(2,1)}, u32[]{:S(2)}) %copy-start.2) | copy-done | bytes 262168
  3.6 0.0 copy-start.3
  3.6 0.7 %copy-done.3 = f32[1,1,1024,6]{2,1,3,0:T(1,128)S(1)} copy-done((f32[1,1,1024,6]{2,1,3,0:T(1,128)S(1)}, f32[1,1,1024,6]{2,1,3,0:T(1,128)}, u32[]{:S(2)}) %copy-start.3) | copy-done | bytes 24600
  4.3 0.0 copy-start.4
  4.3 0.7 %copy-done.4 = f32[1,1,1024]{2,1,0:T(1,128)S(1)} copy-done((f32[1,1,1024]{2,1,0:T(1,128)S(1)}, f32[1,1,1024]{2,1,0:T(1,128)}, u32[]{:S(2)}) %copy-start.4) | copy-done | bytes 4120
  5.0 0.0 copy-start.5
  5.0 0.7 %copy-done.5 = f32[1,1,1024]{2,1,0:T(1,128)S(1)} copy-done((f32[1,1,1024]{2,1,0:T(1,128)S(1)}, f32[1,1,1024]{2,1,0:T(1,128)}, u32[]{:S(2)}) %copy-start.5) | copy-done | bytes 4120
  5.7 0.0 copy-start.6
  5.7 0.7 %copy-done.6 = s32[1,1,1024]{2,1,0:T(1,128)S(1)} copy-done((s32[1,1,1024]{2,1,0:T(1,128)S(1)}, s32[1,1,1024]{2,1,0:T(1,128)}, u32[]{:S(2)}) %copy-start.6) | copy-done | bytes 4120
  6.4 0.0 copy-start.7
  6.4 0.7 %copy-done.7 = s32[1,1,1024]{2,1,0:T(1,128)S(1)} copy-done((s32[1,1,1024]{2,1,0:T(1,128)S(1)}, s32[1,1,1024]{2,1,0:T(1,128)}, u32[]{:S(2)}) %copy-start.7) | copy-done | bytes 4120
  7.1 0.0 copy-start.8
  7.1 0.7 %copy-done.8 = bf16[6,192]{1,0:T(8,128)(2,1)S(1)} copy-done((bf16[6,192]{1,0:T(8,128)(2,1)S(1)}, bf16[6,192]{1,0:T(8,128)(2,1)}, u32[]{:S(2)}) %copy-start.8) | copy-done | bytes 2328
  7.8 14.0 %shard_map.91 = (f32[1024,128]{1,0:T(8,128)S(1)}, bf16[1024,128]{1,0:T(8,128)(2,1)S(1)}, bf16[128,128]{1,0:T(8,128)(2,1)S(1)}) custom-call(bf16[1024,128]{1,0:T(8,128)(2,1)S(1)} %bitcast.13, f32[1024,128]{1,0:T(8,128)S(1)} %bitcast.12, bf16[1024,1024]{1,0:T(8,128)(2,1)S(1)} %bitcast.11, f32[8,128]{1,0:T(8,128)S(1)} %bitcast.15, f32[8,128]{1,0:T(8,128)S(1)} %bitcast.16, ...), custom_call_target="tpu_custom_call" | custom-call | tf_op jit(solution)/shard_map/pallas_call | solution.py:285
  21.8 1.0 %shard_map.92 = f32[1024,128]{1,0:T(8,128)} custom-call(f32[1024,128]{1,0:T(8,128)S(1)} %get-tuple-element.8.total, bf16[1024,128]{1,0:T(8,128)(2,1)S(1)} %get-tuple-element.9.lift, bf16[128,128]{1,0:T(8,128)(2,1)S(1)} %get-tuple-element.10.stack), custom_call_target="tpu_custom_call" | custom-call | tf_op jit(solution)/shard_map/pallas_call | solution.py:299
Async XLA Ops:
  0.0 1.6 %copy-start = (bf16[1,1,1024,1024]{3,2,1,0:T(8,128)(2,1)S(1)}, bf16[1,1,1024,1024]{3,2,1,0:T(8,128)(2,1)}, u32[]{:S(2)}) copy-start(bf16[1,1,1024,1024]{3,2,1,0:T(8,128)(2,1)} %param.11) | copy-start | bytes 6291460
  1.6 1.0 %copy-start.1 = (f32[1,1,1024,128]{3,2,1,0:T(8,128)S(1)}, f32[1,1,1024,128]{3,2,1,0:T(8,128)}, u32[]{:S(2)}) copy-start(f32[1,1,1024,128]{3,2,1,0:T(8,128)} %param.10) | copy-start | bytes 1572868
  2.6 0.9 %copy-start.2 = (bf16[1,1,1024,128]{3,2,1,0:T(8,128)(2,1)S(1)}, bf16[1,1,1024,128]{3,2,1,0:T(8,128)(2,1)}, u32[]{:S(2)}) copy-start(bf16[1,1,1024,128]{3,2,1,0:T(8,128)(2,1)} %param.9) | copy-start | bytes 786436
  3.6 0.7 %copy-start.3 = (f32[1,1,1024,6]{2,1,3,0:T(1,128)S(1)}, f32[1,1,1024,6]{2,1,3,0:T(1,128)}, u32[]{:S(2)}) copy-start(f32[1,1,1024,6]{2,1,3,0:T(1,128)} %param.16) | copy-start | bytes 73732
  4.3 0.7 %copy-start.4 = (f32[1,1,1024]{2,1,0:T(1,128)S(1)}, f32[1,1,1024]{2,1,0:T(1,128)}, u32[]{:S(2)}) copy-start(f32[1,1,1024]{2,1,0:T(1,128)} %param.12) | copy-start | bytes 12292
  5.0 0.7 %copy-start.5 = (f32[1,1,1024]{2,1,0:T(1,128)S(1)}, f32[1,1,1024]{2,1,0:T(1,128)}, u32[]{:S(2)}) copy-start(f32[1,1,1024]{2,1,0:T(1,128)} %param.13) | copy-start | bytes 12292
  5.7 0.7 %copy-start.6 = (s32[1,1,1024]{2,1,0:T(1,128)S(1)}, s32[1,1,1024]{2,1,0:T(1,128)}, u32[]{:S(2)}) copy-start(s32[1,1,1024]{2,1,0:T(1,128)} %param.14) | copy-start | bytes 12292
  6.4 0.7 %copy-start.7 = (s32[1,1,1024]{2,1,0:T(1,128)S(1)}, s32[1,1,1024]{2,1,0:T(1,128)}, u32[]{:S(2)}) copy-start(s32[1,1,1024]{2,1,0:T(1,128)} %param.15) | copy-start | bytes 12292
  7.1 0.7 %copy-start.8 = (bf16[6,192]{1,0:T(8,128)(2,1)S(1)}, bf16[6,192]{1,0:T(8,128)(2,1)}, u32[]{:S(2)}) copy-start(bf16[6,192]{1,0:T(8,128)(2,1)} %cinv_h.1) | copy-start | bytes 6916

commit v4 on v3

--- a/solution.py
+++ b/solution.py
@@ -10,6 +10,7 @@
 MESH = pl.DeviceIdType.MESH
 LANES = 128
 SLOT = 8
+VMEM_BYTES = 67043328
 
 
 def one_hot(mask):
@@ -21,15 +22,23 @@
     return high, (values - high.astype(jnp.float32)).astype(jnp.bfloat16)
 
 
-def peer_offsets(nx, ny):
-    offsets = [(a, b) for a in range(nx) for b in range(ny) if a or b]
-    return sorted(offsets, key=lambda o: abs(o[1] - ny // 2))
+def flipped(index, bits):
+    result = index
+    bit = 1
+    while bit <= bits:
+        if bits & bit:
+            result = result + bit * (1 - 2 * lax.rem(index // bit, 2))
+        bit *= 2
+    return result
 
 
 def for_each_peer(nx, ny, ix, iy, action):
-    if nx * ny <= 64:
-        for a, b in peer_offsets(nx, ny):
-            action(lax.rem(ix + a, nx), lax.rem(iy + b, ny))
+    if nx * ny <= 64 and nx & (nx - 1) == 0 and ny & (ny - 1) == 0:
+        for b in reversed(range(ny)):
+            py = flipped(iy, b)
+            for a in reversed(range(nx)):
+                if a or b:
+                    action(flipped(ix, a), py)
         return
 
     def step(offset, carry):
@@ -86,6 +95,7 @@
     fetch = [pltpu.make_async_copy(a, b, in_sem.at[i]) for i, (a, b) in enumerate(pairs)]
     for copy in fetch:
         copy.start()
+    gathered[...] = jnp.zeros_like(gathered)
     barrier = pltpu.get_barrier_semaphore()
     greeted = greet_row(nx, ix, iy, barrier)
     greeted += greet_column(ny, ix, iy, barrier, 1) + greet_column(ny, ix, iy, barrier, 2)
@@ -195,8 +205,8 @@
 
     def send_coarse(px, py):
         pltpu.make_async_remote_copy(
-            src_ref=coarse_send,
-            dst_ref=gathered.at[me],
+            src_ref=coarse_send.at[pl.ds(0, modes_count)],
+            dst_ref=gathered.at[me, pl.ds(0, modes_count)],
             send_sem=coarse_ssem,
             recv_sem=coarse_rsem,
             device_id=(px, py),
@@ -224,7 +234,7 @@
 
     for copy, exists in sends:
         pl.when(exists)(copy.wait_send)
-    everyone = gathered.at[pl.ds(0, n - 1)]
+    everyone = gathered.at[pl.ds(0, n - 1), pl.ds(0, modes_count)]
     pltpu.make_async_copy(everyone, everyone, coarse_ssem).wait()
     pltpu.make_async_copy(everyone, everyone, coarse_rsem).wait()
 
@@ -280,6 +290,7 @@
         pltpu.SemaphoreType.DMA,
         pltpu.SemaphoreType.REGULAR((len(column_reaches(ny)) + 1,)),
     ]
+    kept = m * k * 4 + m * LANES * 2 + LANES * k * 2
     vmem = pl.BlockSpec(memory_space=pltpu.VMEM)
     anywhere = pl.BlockSpec(memory_space=pl.ANY)
     parts = pl.pallas_call(
@@ -289,11 +300,11 @@
             pltpu.VMEM((m, LANES), jnp.bfloat16),
             pltpu.VMEM((LANES, k), jnp.bfloat16),
         ),
-        in_specs=[pl.BlockSpec(memory_space=pltpu.HBM)] * len(operands),
+        in_specs=[anywhere] * len(operands),
         out_specs=[vmem] * 3,
         scratch_shapes=scratch,
         compiler_params=pltpu.CompilerParams(
-            collective_id=0, has_side_effects=True, vmem_limit_bytes=40 << 20
+            collective_id=0, has_side_effects=True, vmem_limit_bytes=VMEM_BYTES - kept - (64 << 10)
         ),
     )(*operands)
     result = pl.pallas_call(

time: 23.3 us -> 14.8 us (0.64); the launches traced: 22.8 us -> 14.7 us
  local copies, waits for them, and re-layouts: 7.75 us -> 0 us
  Pallas kernels: 15 us -> 14.7 us
    unnamed x18 -> x0, local copies, waits for them, and re-layouts: 7.75 us -> none
    pallas_call x1, Pallas kernels: 14 us -> 13.6 us  [body(): pl.pallas_call(functools.partial(kernel, nx, ny, modes_count), out_shape=...]
where the time goes in v4:
time: 14.8 us; the launch traced here: 14.7 us
  Pallas kernels  14.7 us (99%)
    pallas_call x1, Pallas kernels, body(): pl.pallas_call(functools.partial(kernel, nx, ny, modes_count), out_shape=...  13.6 us
    pallas_call x1, Pallas kernels, body(): pl.pallas_call(finish, out_shape=jax.ShapeDtypeStruct((m, k), jnp.float32...  1.01 us

profile of v4, /device:TPU:0, one launch (start us, length us, event | category | flops | bytes accessed | tf_op | source)
XLA Modules:
  0.0 14.7 jit_solution(9163083270775130103)
XLA Ops:
  0.0 13.6 %shard_map.91 = (f32[1024,128]{1,0:T(8,128)S(1)}, bf16[1024,128]{1,0:T(8,128)(2,1)S(1)}, bf16[128,128]{1,0:T(8,128)(2,1)S(1)}) custom-call(bf16[1024,128]{1,0:T(8,128)(2,1)} %bitcast.13, f32[1024,128]{1,0:T(8,128)} %bitcast.12, bf16[1024,1024]{1,0:T(8,128)(2,1)} %bitcast.11, f32[8,128]{1,0:T(8,128)} %bitcast.15, f32[8,128]{1,0:T(8,128)} %bitcast.16, ...), custom_call_target="tpu_custom_call" | custom-call | tf_op jit(solution)/shard_map/pallas_call | solution.py:296
  13.7 1.0 %shard_map.92 = f32[1024,128]{1,0:T(8,128)} custom-call(f32[1024,128]{1,0:T(8,128)S(1)} %get-tuple-element.8.total, bf16[1024,128]{1,0:T(8,128)(2,1)S(1)} %get-tuple-element.9.lift, bf16[128,128]{1,0:T(8,128)(2,1)S(1)} %get-tuple-element.10.stack), custom_call_target="tpu_custom_call" | custom-call | tf_op jit(solution)/shard_map/pallas_call | solution.py:310

commit v5 on v4

--- a/solution.py
+++ b/solution.py
@@ -76,9 +76,9 @@
 def kernel(
     nx, ny, modes_count,
     loads_h, guess_h, inverse_h, diag_h, coup_h, rows_h, owned_h, modes_h, cinv_h,
-    total, lift, stack_out,
+    total, weights, coarse_all,
     loads, guess, inverse, diag, coup, rows, owned, modes, cinv,
-    halo_send, halo_recv, place, base, gathered, coarse_send, spread,
+    halo_send, halo_recv, place, base, gathered, coarse_send,
     in_sem, halo_ssem, halo_rsem, coarse_ssem, coarse_rsem, ready,
 ):
     n = nx * ny
@@ -171,26 +171,6 @@
         precision=lax.Precision.HIGHEST, preferred_element_type=jnp.float32,
     )
 
-    fetch[6].wait()
-    group = min(n, 64)
-    narrow, wide = group * modes_count, group * SLOT
-    wide_at = lax.broadcasted_iota(jnp.int32, (narrow, wide), 1)
-    slot_row = lax.rem(wide_at, SLOT)
-    source_row = lax.div(wide_at, SLOT) * modes_count + slot_row
-    narrow_at = lax.broadcasted_iota(jnp.int32, (narrow, wide), 0)
-    expand = one_hot((narrow_at == source_row) & (slot_row < modes_count))
-    for g in range(n // group):
-        spread[:, g * wide : (g + 1) * wide] = jnp.dot(
-            cinv[:, g * narrow : (g + 1) * narrow], expand, preferred_element_type=jnp.float32
-        ).astype(jnp.bfloat16)
-    for j in range(chunks):
-        high, low = split(mode_rows[j])
-        high, low = high.astype(jnp.float32), low.astype(jnp.float32)
-        stack = jnp.concatenate(
-            [high, high, low, jnp.zeros((LANES - 3 * SLOT, LANES), jnp.float32)], axis=0
-        )
-        lift[j * LANES : (j + 1) * LANES, :] = stack.T.astype(jnp.bfloat16)
-
     pl.semaphore_wait(ready.at[len(reaches)], expected)
     for side, exists in enumerate((ix > 0, ix < nx - 1, iy > 0, iy < ny - 1)):
         slot = halo_recv.at[side]
@@ -215,6 +195,33 @@
 
     for_each_peer(nx, ny, ix, iy, send_coarse)
 
+    fetch[6].wait()
+    group = min(n, 64)
+    narrow, wide = group * modes_count, group * SLOT
+    wide_at = lax.broadcasted_iota(jnp.int32, (narrow, wide), 1)
+    slot_row = lax.rem(wide_at, SLOT)
+    source_row = lax.div(wide_at, SLOT) * modes_count + slot_row
+    narrow_at = lax.broadcasted_iota(jnp.int32, (narrow, wide), 0)
+    expand = one_hot((narrow_at == source_row) & (slot_row < modes_count))
+    lifts = []
+    for j in range(chunks):
+        high, low = split(mode_rows[j])
+        high, low = high.astype(jnp.float32), low.astype(jnp.float32)
+        stack = jnp.concatenate(
+            [high, low, jnp.zeros((LANES - 2 * SLOT, LANES), jnp.float32)], axis=0
+        )
+        lifts.append(stack.T.astype(jnp.bfloat16))
+    pad = jnp.zeros((SLOT - modes_count, wide), jnp.float32)
+    rest = jnp.zeros((LANES - 2 * SLOT, wide), jnp.float32)
+    for g in range(n // group):
+        spread = jnp.dot(
+            cinv[:, g * narrow : (g + 1) * narrow], expand, preferred_element_type=jnp.float32
+        )
+        stack = jnp.concatenate([spread, pad, spread, pad, rest], axis=0).astype(jnp.bfloat16)
+        for j in range(chunks):
+            weights[j * LANES : (j + 1) * LANES, g * wide : (g + 1) * wide] = jnp.dot(
+                lifts[j], stack, preferred_element_type=jnp.float32
+            ).astype(jnp.bfloat16)
     coup_columns = coup[...].T
     placed = jnp.dot(place[...], received, preferred_element_type=jnp.float32)
     residual_half = []
@@ -238,23 +245,16 @@
     pltpu.make_async_copy(everyone, everyone, coarse_ssem).wait()
     pltpu.make_async_copy(everyone, everyone, coarse_rsem).wait()
 
-    coef = jnp.dot(
-        spread[...], gathered[...].reshape(n * SLOT, k), preferred_element_type=jnp.float32
-    )
-    coef = jnp.concatenate([coef, jnp.zeros((SLOT - modes_count, k), jnp.float32)], axis=0)
-    high, low = split(coef)
-    stack_out[...] = jnp.concatenate(
-        [high, low, high, jnp.zeros((LANES - 3 * SLOT, k), jnp.bfloat16)], axis=0
-    )
-
-
-def finish(total, lift, stack, out_h, staged, out_sem):
+    coarse_all[...] = gathered[...].reshape(n * SLOT, k)
+
+
+def finish(total, weights, coarse_all, out_h, staged, out_sem):
     chunks = total.shape[0] // LANES
     stores = []
     for j in range(chunks):
         at = pl.ds(j * LANES, LANES)
         staged[at, :] = total[at, :] + jnp.dot(
-            lift[at, :], stack[...], preferred_element_type=jnp.float32
+            weights[at, :], coarse_all[...], preferred_element_type=jnp.float32
         )
         copy = pltpu.make_async_copy(staged.at[at], out_h.at[at], out_sem.at[j])
         copy.start()
@@ -282,7 +282,6 @@
         pltpu.VMEM((m, k), jnp.float32),
         pltpu.VMEM((n, SLOT, k), jnp.bfloat16),
         pltpu.VMEM((SLOT, k), jnp.bfloat16),
-        pltpu.VMEM((modes_count, n * SLOT), jnp.bfloat16),
         pltpu.SemaphoreType.DMA((len(operands),)),
         pltpu.SemaphoreType.DMA((4,)),
         pltpu.SemaphoreType.DMA((4,)),
@@ -290,15 +289,15 @@
         pltpu.SemaphoreType.DMA,
         pltpu.SemaphoreType.REGULAR((len(column_reaches(ny)) + 1,)),
     ]
-    kept = m * k * 4 + m * LANES * 2 + LANES * k * 2
+    kept = m * k * 4 + (m + k) * n * SLOT * 2
     vmem = pl.BlockSpec(memory_space=pltpu.VMEM)
     anywhere = pl.BlockSpec(memory_space=pl.ANY)
     parts = pl.pallas_call(
         functools.partial(kernel, nx, ny, modes_count),
         out_shape=(
             pltpu.VMEM((m, k), jnp.float32),
-            pltpu.VMEM((m, LANES), jnp.bfloat16),
-            pltpu.VMEM((LANES, k), jnp.bfloat16),
+            pltpu.VMEM((m, n * SLOT), jnp.bfloat16),
+            pltpu.VMEM((n * SLOT, k), jnp.bfloat16),
         ),
         in_specs=[anywhere] * len(operands),
         out_specs=[vmem] * 3,

time: 14.8 us -> 14.7 us (level)
  Pallas kernels: 14.7 us -> 14.5 us
where the time goes in v5:
time: 14.7 us; the launch traced here: 14.5 us
  Pallas kernels  14.5 us (99%)
    pallas_call x1, Pallas kernels, body(): pl.pallas_call(functools.partial(kernel, nx, ny, modes_count), out_shape=...  13.5 us
    pallas_call x1, Pallas kernels, body(): pl.pallas_call(finish, out_shape=jax.ShapeDtypeStruct((m, k), jnp.float32...  1.03 us

profile of v5, /device:TPU:0, one launch (start us, length us, event | category | flops | bytes accessed | tf_op | source)
XLA Modules:
  0.0 14.5 jit_solution(1681493564190483867)
XLA Ops:
  0.0 13.5 %shard_map.91 = (f32[1024,128]{1,0:T(8,128)S(1)}, bf16[1024,256]{1,0:T(8,128)(2,1)S(1)}, bf16[256,128]{1,0:T(8,128)(2,1)S(1)}) custom-call(bf16[1024,128]{1,0:T(8,128)(2,1)} %bitcast.13, f32[1024,128]{1,0:T(8,128)} %bitcast.12, bf16[1024,1024]{1,0:T(8,128)(2,1)} %bitcast.11, f32[8,128]{1,0:T(8,128)} %bitcast.15, f32[8,128]{1,0:T(8,128)} %bitcast.16, ...), custom_call_target="tpu_custom_call" | custom-call | tf_op jit(solution)/shard_map/pallas_call | solution.py:295
  13.5 1.0 %shard_map.92 = f32[1024,128]{1,0:T(8,128)} custom-call(f32[1024,128]{1,0:T(8,128)S(1)} %get-tuple-element.8.total, bf16[1024,256]{1,0:T(8,128)(2,1)S(1)} %get-tuple-element.9.weights, bf16[256,128]{1,0:T(8,128)(2,1)S(1)} %get-tuple-element.10.coarse_all), custom_call_target="tpu_custom_call" | custom-call | tf_op jit(solution)/shard_map/pallas_call | solution.py:309
